TPU v7x, 128 devices: a whole 4x4x4 slice. The times are simulated.
128 devices in a mesh: grp: 8 (over y, core), dev: 16 (over x, z).
Axes of the slice: x: 4, y: 4, z: 4, core: 2. Of those that a mesh axis runs over, the one named last changes fastest.
Arguments:
- suffix_queries: bfloat16 [16384, 2048], P(('grp', 'dev')), may hold values from -12 to 12
- suffix_keys: bfloat16 [16384, 2048], P(('grp', 'dev')), may hold values from -12 to 12
- suffix_values: bfloat16 [16384, 2048], P(('grp', 'dev')), may hold values from -6 to 6
- layer_input: bfloat16 [16384, 2048], P(('grp', 'dev')), may hold values from -6 to 6
- suffix_lengths: int32 [128, 8], P(('grp', 'dev')), may hold values from 1 to 32, as said below
- request_group: int32 [128, 8], P(('grp', 'dev')), may hold values from 0 to 7, as said below
- prefix_keys: bfloat16 [8, 4096, 2048], P('grp', None, 'dev'), may hold values from -12 to 12
- prefix_values: bfloat16 [8, 4096, 2048], P('grp', None, 'dev'), may hold values from -6 to 6
- up_weight: bfloat16 [2048, 8192], P(None, ('grp', 'dev')), may hold values from -0.125 to 0.125
- up_bias: bfloat16 [8192], P(('grp', 'dev')), may hold values from -3 to 3
- down_weight: bfloat16 [8192, 2048], P(('grp', 'dev')), may hold values from -0.0625 to 0.0625
- down_bias: float32 [2048], replicated, may hold values from -3 to 3
- attn_gain: float32 [2048], replicated, may hold values from 0.5 to 1.5
- attn_shift: float32 [2048], replicated, may hold values from -2 to 2
- out_gain: float32 [2048], replicated, may hold values from 0.5 to 1.5
- out_shift: float32 [2048], replicated, may hold values from -2 to 2
Outputs:
- layer_output: bfloat16 [16384, 2048], P(('grp', 'dev'))
Inputs may be any that keep to these rules, and one draw needn't show every extreme that they name: `suffix_lengths`: each row lists one device's 8 requests in slot order; they fill its 128 slots exactly, and at least one of them has 32 tokens. `request_group`: the 8 requests of one row name every prefix exactly once.
All inputs are finite; a program needn't handle non-finite values.
Results may differ from a plain program's by a relative error of at most 0.014.
Values may be sent and summed in bfloat16 or wider, within the bound.
A program may use at most 128 MiB of HBM per device.

v0:
```python
import math
import jax
import jax.numpy as jnp
from jax import lax
from jax.sharding import PartitionSpec as P

HD = 128
norm_eps = 1e-12


def layer_norm(summed, norm_gain, norm_shift):
    row_mean = jnp.mean(summed, axis=-1, keepdims=True)
    centred = summed - row_mean
    spread = jnp.mean(centred * centred, axis=-1, keepdims=True)
    return centred * lax.rsqrt(spread + norm_eps) * norm_gain + norm_shift


def request_layout(lengths, slot_count):
    end_points = jnp.cumsum(lengths)
    starts = end_points - lengths
    positions = lax.iota(jnp.int32, slot_count)
    member = (positions[:, None] >= starts[None, :]) & (positions[:, None] < end_points[None, :])
    slot_ids = lax.iota(jnp.int32, lengths.shape[0])
    segment = jnp.sum(jnp.where(member, slot_ids[None, :], 0), axis=1)
    return (starts, segment)


def expand_rows(piece_rows, up_matrix, up_offset):
    product = jnp.dot(piece_rows, up_matrix, preferred_element_type=jnp.float32)
    return jax.nn.gelu(product + up_offset.astype(jnp.float32), approximate=True).astype(
        jnp.bfloat16
    )


def attend_prefix(arrived, cache_keys, cache_values):
    sources, row_count, part_width = arrived.shape
    local_heads = part_width // HD
    per_block = math.gcd(sources, max(1, 512 // row_count))
    query_blocks = arrived.reshape(sources // per_block, per_block * row_count, local_heads, HD)
    key_heads = cache_keys.reshape(-1, local_heads, HD)
    value_heads = cache_values.reshape(-1, local_heads, HD)

    def one_block(query_block):
        scores = jnp.einsum(
            "qhd,khd->hqk", query_block, key_heads, preferred_element_type=jnp.float32
        ) * HD ** (-0.5)
        row_top = jnp.max(scores, axis=2).astype(jnp.bfloat16)
        weights = jnp.exp(
            scores - lax.optimization_barrier(row_top).astype(jnp.float32)[:, :, None]
        )
        row_sum = jnp.sum(weights, axis=2)
        mixed_sum = jnp.einsum(
            "hqk,khd->qhd",
            weights.astype(jnp.bfloat16),
            value_heads,
            preferred_element_type=jnp.float32,
        )
        answer = (mixed_sum / row_sum.T[:, :, None]).astype(jnp.bfloat16)
        return (answer.reshape(-1, part_width), row_top.T, row_sum.T.astype(jnp.bfloat16))

    answer, row_top, row_sum = lax.map(one_block, query_blocks)
    return (
        answer.reshape(sources, row_count, part_width),
        row_top.reshape(sources, row_count, local_heads),
        row_sum.reshape(sources, row_count, local_heads),
    )


def attend_suffix(query_rows, key_rows, value_rows, segment, head_count):
    slot_count = query_rows.shape[0]
    query_heads = query_rows.reshape(slot_count, head_count, HD)
    key_heads = key_rows.reshape(slot_count, head_count, HD)
    value_heads = value_rows.reshape(slot_count, head_count, HD)
    scores = jnp.einsum(
        "qhd,khd->hqk", query_heads, key_heads, preferred_element_type=jnp.float32
    ) * HD ** (-0.5)
    positions = lax.iota(jnp.int32, slot_count)
    visible = ((segment[:, None] == segment[None, :]) & (positions[None, :] <= positions[:, None]))[
        None
    ]
    row_top = jnp.max(jnp.where(visible, scores, -jnp.inf), axis=2)
    weights = jnp.where(visible, jnp.exp(scores - row_top[:, :, None]), 0.0)
    row_sum = jnp.sum(weights, axis=2)
    mixed_sum = jnp.einsum(
        "hqk,khd->qhd",
        weights.astype(jnp.bfloat16),
        value_heads,
        preferred_element_type=jnp.float32,
    )
    return (row_top.T, row_sum.T, mixed_sum)


def merge_parts(far_answer, far_top, far_sum, own_top, own_sum, own_mixed):
    far_top = far_top.astype(jnp.float32)
    far_sum = far_sum.astype(jnp.float32)
    joint_top = jnp.maximum(far_top, own_top)
    far_weight = jnp.exp(far_top - joint_top) * far_sum
    own_weight = jnp.exp(own_top - joint_top)
    numerator = (
        far_weight[:, :, None] * far_answer.astype(jnp.float32) + own_weight[:, :, None] * own_mixed
    )
    return numerator / (far_weight + own_weight * own_sum)[:, :, None]


def on_device(
    suffix_queries,
    suffix_keys,
    suffix_values,
    layer_input,
    suffix_lengths,
    request_group,
    prefix_keys,
    prefix_values,
    up_weight,
    up_bias,
    down_weight,
    down_bias,
    attn_gain,
    attn_shift,
    out_gain,
    out_shift,
):
    slot_count, model_width = suffix_queries.shape
    head_count = model_width // HD
    group_count = lax.axis_size("grp")
    column_count = lax.axis_size("dev")
    part_width = model_width // column_count
    local_heads = part_width // HD
    capacity = 2 * slot_count // group_count
    lengths = suffix_lengths[0]
    groups = request_group[0]
    request_total = lengths.shape[0]
    starts, segment = request_layout(lengths, slot_count)
    anchor = jnp.zeros((), jnp.int32)
    padded = jnp.concatenate(
        [suffix_queries, jnp.zeros((capacity, model_width), jnp.bfloat16)], axis=0
    )
    slot_rank = lax.iota(jnp.int32, capacity)
    outgoing = jnp.zeros((group_count, column_count, capacity, part_width), jnp.bfloat16)
    for request in range(request_total):
        taken = lax.dynamic_slice_in_dim(padded, starts[request], capacity, 0)
        taken = jnp.where((slot_rank < lengths[request])[:, None], taken, jnp.zeros_like(taken))
        split_rows = taken.reshape(capacity, column_count, part_width).transpose(1, 0, 2)
        outgoing = lax.dynamic_update_slice(
            outgoing, split_rows[None], (groups[request], anchor, anchor, anchor)
        )
    cache_keys = prefix_keys[0]
    cache_values = prefix_values[0]
    answer_part, top_part, sum_part = attend_prefix(
        lax.all_to_all(
            outgoing.reshape(group_count * column_count, capacity, part_width),
            ("grp", "dev"),
            split_axis=0,
            concat_axis=0,
            tiled=True,
        ),
        cache_keys,
        cache_values,
    )
    answer = lax.all_to_all(answer_part, ("grp", "dev"), split_axis=0, concat_axis=0, tiled=True)
    far_top = lax.all_to_all(top_part, ("grp", "dev"), split_axis=0, concat_axis=0, tiled=True)
    far_sum = lax.all_to_all(sum_part, ("grp", "dev"), split_axis=0, concat_axis=0, tiled=True)
    answer = answer.reshape(group_count, column_count, capacity, part_width)
    far_top = far_top.reshape(group_count, column_count, capacity, local_heads)
    far_sum = far_sum.reshape(group_count, column_count, capacity, local_heads)
    placed_answer = jnp.zeros((slot_count + capacity, model_width), jnp.bfloat16)
    placed_top = jnp.zeros((slot_count + capacity, head_count), jnp.bfloat16)
    placed_sum = jnp.zeros((slot_count + capacity, head_count), jnp.bfloat16)
    for request in range(request_total):
        own_answer = (
            lax.dynamic_index_in_dim(answer, groups[request], 0, keepdims=False)
            .transpose(1, 0, 2)
            .reshape(capacity, model_width)
        )
        own_top_rows = (
            lax.dynamic_index_in_dim(far_top, groups[request], 0, keepdims=False)
            .transpose(1, 0, 2)
            .reshape(capacity, head_count)
        )
        own_sum_rows = (
            lax.dynamic_index_in_dim(far_sum, groups[request], 0, keepdims=False)
            .transpose(1, 0, 2)
            .reshape(capacity, head_count)
        )
        placed_answer = lax.dynamic_update_slice(
            placed_answer, own_answer, (starts[request], anchor)
        )
        placed_top = lax.dynamic_update_slice(placed_top, own_top_rows, (starts[request], anchor))
        placed_sum = lax.dynamic_update_slice(placed_sum, own_sum_rows, (starts[request], anchor))
    own_top, own_sum, own_mixed = attend_suffix(
        suffix_queries, suffix_keys, suffix_values, segment, head_count
    )
    far_rows = placed_answer[:slot_count].reshape(slot_count, head_count, HD)
    context = merge_parts(
        far_rows, placed_top[:slot_count], placed_sum[:slot_count], own_top, own_sum, own_mixed
    )
    hidden_state = layer_norm(
        layer_input.astype(jnp.float32) + context.reshape(slot_count, model_width),
        attn_gain,
        attn_shift,
    ).astype(jnp.bfloat16)
    up_slice, bias_slice, down_slice = (
        lax.all_gather(up_weight, "grp", axis=1, tiled=True),
        lax.all_gather(up_bias, "grp", axis=0, tiled=True),
        lax.all_gather(down_weight, "grp", axis=0, tiled=True),
    )
    activation = expand_rows(
        lax.all_gather(hidden_state, "dev", axis=0, tiled=True), up_slice, bias_slice
    )
    mlp_sum = lax.psum_scatter(
        jnp.dot(activation, down_slice, preferred_element_type=jnp.float32).astype(jnp.bfloat16),
        "dev",
        scatter_dimension=0,
        tiled=True,
    ).astype(jnp.float32)
    return layer_norm(
        hidden_state.astype(jnp.float32) + mlp_sum + down_bias, out_gain, out_shift
    ).astype(jnp.bfloat16)


def solution(mesh):
    placed = (
        P(("grp", "dev"), None),
        P(("grp", "dev"), None),
        P(("grp", "dev"), None),
        P(("grp", "dev"), None),
        P(("grp", "dev"), None),
        P(("grp", "dev"), None),
        P("grp", None, "dev"),
        P("grp", None, "dev"),
        P(None, ("grp", "dev")),
        P(("grp", "dev")),
        P(("grp", "dev"), None),
        P(),
        P(),
        P(),
        P(),
        P(),
    )
    return jax.shard_map(
        on_device, mesh=mesh, in_specs=placed, out_specs=P(("grp", "dev"), None), check_vma=False
    )
```

profile of v0, /device:TPU:0, one launch (start us, length us, event | category | flops | bytes accessed | tf_op | source)
XLA Modules:
  0.0 412.4 jit_solution(14731411691771604662)
XLA Ops:
  7.3 0.8 reduce-window.4
  19.4 1.6 fusion.105
  31.0 1.6 fusion.103
  47.8 1.1 fusion.62
  48.9 1.2 broadcast_in_dim.147
  50.7 1.7 fusion.64
  57.2 11.2 %all-to-all-start = ((bf16[128,32,128]{2,1,0:T(8,128)(2,1)}), bf16[128,32,128]{2,1,0:T(8,128)(2,1)S(1)}, u32[]{:S(2)}, u32[]{:S(2)}) async-start(bf16[128,32,128]{2,1,0:T(8,128)(2,1)} %bitcast.51), calls=%async_computation | async-start | bytes 2097152 | tf_op jit(solution)/shard_map/all_to_all | solution.py:150
  69.2 18.3 %all-to-all-done = bf16[128,32,128]{2,1,0:T(8,128)(2,1)S(1)} async-done(((bf16[128,32,128]{2,1,0:T(8,128)(2,1)}), bf16[128,32,128]{2,1,0:T(8,128)(2,1)S(1)}, u32[]{:S(2)}, u32[]{:S(2)}) %all-to-all-start) | async-done | bytes 1048608 | tf_op jit(solution)/shard_map/all_to_all | solution.py:150
  87.5 41.1 %while.14 = (s32[]{:T(128)}, bf16[8,512,128]{2,1,0:T(8,128)(2,1)}, bf16[8,512,1]{1,0,2:T(8,128)(2,1)S(1)}, bf16[8,512,1]{1,0,2:T(8,128)(2,1)S(1)}, bf16[8,512,1,...) while((s32[]{:T(128)}, bf16[8,512,128]{2,1,0:T(8,128)(2,1)}, ...), condition=%wide.region_4.5_spmd, body=%wide.region_1.4_spmd.sunk | while | flops 1090650112 | bytes 31745168 | solution.py:61
  87.5 1.3 multiply_reduce_fusion.4
  88.9 1.5 fusion.118
  90.4 2.1 fusion.119
  92.6 1.3 multiply_reduce_fusion.4
  94.0 1.5 fusion.118
  95.5 2.2 fusion.119
  97.8 1.3 multiply_reduce_fusion.4
  99.2 1.5 fusion.118
  100.7 2.1 fusion.119
  102.9 1.3 multiply_reduce_fusion.4
  104.3 1.5 fusion.118
  105.8 2.1 fusion.119
  108.0 1.3 multiply_reduce_fusion.4
  109.4 1.5 fusion.118
  110.9 2.1 fusion.119
  113.2 1.3 multiply_reduce_fusion.4
  114.6 1.5 fusion.118
  116.1 2.1 fusion.119
  118.3 1.3 multiply_reduce_fusion.4
  119.7 1.5 fusion.118
  121.2 2.1 fusion.119
  123.4 1.3 multiply_reduce_fusion.4
  124.8 1.5 fusion.118
  126.3 2.2 fusion.119
  129.3 4.6 %all-to-all-start.2 = ((bf16[128,32,1]{1,2,0:T(2,128)(2,1)}), bf16[128,32,1]{1,2,0:T(2,128)(2,1)S(1)}, u32[]{:S(2)}, u32[]{:S(2)}) async-start(bf16[128,32,1]{1,2,0:T(2,128)(2,1)} %reshape.401), calls=%async_computation.2 | async-start | bytes 131072 | tf_op jit(solution)/shard_map/all_to_all | solution.py:162
  134.6 8.8 %all-to-all-done.2 = bf16[128,32,1]{1,2,0:T(2,128)(2,1)S(1)} async-done(((bf16[128,32,1]{1,2,0:T(2,128)(2,1)}), bf16[128,32,1]{1,2,0:T(2,128)(2,1)S(1)}, u32[]{:S(2)}, u32[]{:S(2)}) %all-to-all-start.2) | async-done | bytes 8224 | tf_op jit(solution)/shard_map/all_to_all | solution.py:162
  143.4 4.6 %all-to-all-start.1 = ((bf16[128,32,1]{1,2,0:T(2,128)(2,1)}), bf16[128,32,1]{1,2,0:T(2,128)(2,1)S(1)}, u32[]{:S(2)}, u32[]{:S(2)}) async-start(bf16[128,32,1]{1,2,0:T(2,128)(2,1)} %reshape.400), calls=%async_computation.1 | async-start | bytes 131072 | tf_op jit(solution)/shard_map/all_to_all | solution.py:161
  148.0 9.4 %all-to-all-done.1 = bf16[128,32,1]{1,2,0:T(2,128)(2,1)S(1)} async-done(((bf16[128,32,1]{1,2,0:T(2,128)(2,1)}), bf16[128,32,1]{1,2,0:T(2,128)(2,1)S(1)}, u32[]{:S(2)}, u32[]{:S(2)}) %all-to-all-start.1) | async-done | bytes 8224 | tf_op jit(solution)/shard_map/all_to_all | solution.py:161
  157.4 4.6 %all-to-all-start.3 = ((bf16[128,32,128]{2,1,0:T(8,128)(2,1)}), bf16[128,32,128]{2,1,0:T(8,128)(2,1)S(1)}, u32[]{:S(2)}, u32[]{:S(2)}) async-start(bf16[128,32,128]{2,1,0:T(8,128)(2,1)} %bitcast.380), calls=%async_computation.3 | async-start | bytes 2097152 | tf_op jit(solution)/shard_map/all_to_all | solution.py:160
  162.1 2.0 copy.149
  164.8 1.0 copy-done.5
  170.3 10.7 %all-to-all-done.3 = bf16[128,32,128]{2,1,0:T(8,128)(2,1)S(1)} async-done(((bf16[128,32,128]{2,1,0:T(8,128)(2,1)}), bf16[128,32,128]{2,1,0:T(8,128)(2,1)S(1)}, u32[]{:S(2)}, u32[]{:S(2)}) %all-to-all-start.3) | async-done | bytes 1048608 | tf_op jit(solution)/shard_map/all_to_all | solution.py:160
  182.0 1.1 copy.141
  183.1 1.0 copy.140
  184.1 1.0 copy.139
  185.1 1.0 copy.138
  186.2 1.0 copy.137
  187.3 4.9 %dynamic_update_slice.131 = bf16[160,2048]{0,1:T(8,128)(2,1)S(1)} dynamic-update-slice(bf16[160,2048]{0,1:T(8,128)(2,1)S(1)} %broadcast_in_dim.168, bf16[32,2048]{0,1:T(8,128)(2,1)} %bitcast.379, s32[]{:T(128)S(6)} %select_n.134, s32[]{:T(128)} %constant.96.clone.1) | dynamic-update-slice | bytes 262148 | tf_op jit(solution)/shard_map/dynamic_update_slice | solution.py:185
  192.2 5.9 %dynamic_update_slice.132 = bf16[160,2048]{0,1:T(8,128)(2,1)S(1)} dynamic-update-slice(bf16[160,2048]{0,1:T(8,128)(2,1)S(1)} %dynamic_update_slice.131, bf16[32,2048]{0,1:T(8,128)(2,1)} %bitcast.378, s32[]{:T(128)S(6)} %select_n.137, s32[]{:T(128)} %constant.96.clone.1) | dynamic-update-slice | bytes 262148 | tf_op jit(solution)/shard_map/dynamic_update_slice | solution.py:185
  198.1 5.9 %dynamic_update_slice.133 = bf16[160,2048]{0,1:T(8,128)(2,1)S(1)} dynamic-update-slice(bf16[160,2048]{0,1:T(8,128)(2,1)S(1)} %dynamic_update_slice.132, bf16[32,2048]{0,1:T(8,128)(2,1)} %bitcast.377, s32[]{:T(128)S(6)} %select_n.140, s32[]{:T(128)} %constant.96.clone.1) | dynamic-update-slice | bytes 262148 | tf_op jit(solution)/shard_map/dynamic_update_slice | solution.py:185
  204.1 5.9 %dynamic_update_slice.134 = bf16[160,2048]{0,1:T(8,128)(2,1)S(1)} dynamic-update-slice(bf16[160,2048]{0,1:T(8,128)(2,1)S(1)} %dynamic_update_slice.133, bf16[32,2048]{0,1:T(8,128)(2,1)} %bitcast.376, s32[]{:T(128)S(6)} %select_n.143, s32[]{:T(128)} %constant.96.clone.1) | dynamic-update-slice | bytes 262148 | tf_op jit(solution)/shard_map/dynamic_update_slice | solution.py:185
  210.0 5.9 %dynamic_update_slice.135 = bf16[160,2048]{0,1:T(8,128)(2,1)S(1)} dynamic-update-slice(bf16[160,2048]{0,1:T(8,128)(2,1)S(1)} %dynamic_update_slice.134, bf16[32,2048]{0,1:T(8,128)(2,1)} %bitcast.375, s32[]{:T(128)S(6)} %select_n.146, s32[]{:T(128)} %constant.96.clone.1) | dynamic-update-slice | bytes 262148 | tf_op jit(solution)/shard_map/dynamic_update_slice | solution.py:185
  216.0 4.0 dynamic_update_slice.136
  220.0 4.0 dynamic_update_slice.137
  224.0 4.2 %dynamic_update_slice.138 = bf16[160,2048]{0,1:T(8,128)(2,1)S(1)} dynamic-update-slice(bf16[160,2048]{0,1:T(8,128)(2,1)S(1)} %dynamic_update_slice.137, bf16[32,2048]{0,1:T(8,128)(2,1)S(1)} %bitcast.372, s32[]{:T(128)S(6)} %select_n.155, s32[]{:T(128)} %constant.96.clone.1) | dynamic-update-slice | bytes 262148 | tf_op jit(solution)/shard_map/dynamic_update_slice | solution.py:185
  228.3 2.8 fusion.36
  231.1 1.6 copy.147
  233.3 1.1 add_convert_fusion.1
  235.9 12.8 %all-reduce.1 = bf16[512]{0:T(512)(128)(2,1)S(1)} all-reduce(bf16[512]{0:T(512)(128)(2,1)S(1)} %dynamic-update-slice), channel_id=1, replica_groups=mesh['grp'=8,'dev'=16] {'grp'}, use_global_device_ids=true, to_apply=%add.1 | all-reduce | flops 512 | bytes 2048
  248.8 52.0 %all-gather.4.cloned.1.call-done = bf16[2048,2048]{1,0:T(8,128)(2,1)} async-done(((bf16[128,2048]{1,0:T(8,128)(2,1)}), bf16[2048,2048]{1,0:T(8,128)(2,1)}) %all-gather.4.cloned.1.call-update) | async-done | bytes 8388624 | tf_op jit(solution)/shard_map/all_gather | solution.py:208
  300.8 15.2 %convolution_convert_fusion = bf16[2048,2048]{1,0:T(8,128)(2,1)} fusion(bf16[512,2048]{1,0:T(8,128)(2,1)} %all-gather.8.cloned.1.call-done, bf16[2048,2048]{1,0:T(8,128)(2,1)} %all-gather.4.cloned.1.call-done, bf16[2048,512]{0,1:T(8,128)(2,1)} %all-gather.6.cloned.1.call-done, f32[512]{0:T(512)S(1)} %convert_element_type.97), kind=kOutput, calls=%fused_computation.17 | convolution fusion | flops 8604614656 | bytes 20973568 | tf_op jit(solution)/shard_map/dot_general | solution.py:211
  316.1 84.9 %reduce-scatter.2.cloned.1.call-done = bf16[128,2048]{1,0:T(8,128)(2,1)} async-done(((bf16[2048,2048]{1,0:T(8,128)(2,1)}), bf16[128,2048]{1,0:T(8,128)(2,1)}) %reduce-scatter.2.cloned.1.call-update) | async-done | bytes 524304 | tf_op jit(solution)/shard_map/reduce_scatter | solution.py:210
  401.0 1.3 fusion.39
  402.3 1.4 multiply_reduce_fusion.1
  403.7 2.2 add_convert_fusion
  (175 shorter events, 23.5 us)
Async XLA Ops:
  6.5 157.7 %copy-start = (bf16[128,2048]{1,0:T(8,128)(2,1)S(1)}, bf16[128,2048]{1,0:T(8,128)(2,1)}, u32[]{:S(2)}) copy-start(bf16[128,2048]{1,0:T(8,128)(2,1)} %param.19) | copy-start | bytes 1572868
  6.5 80.9 %copy-start.1 = (bf16[1,4096,128]{2,1,0:T(8,128)(2,1)S(1)}, bf16[1,4096,128]{2,1,0:T(8,128)(2,1)}, u32[]{:S(2)}) copy-start(bf16[1,4096,128]{2,1,0:T(8,128)(2,1)} %param.24) | copy-start | bytes 3145732
  6.5 242.2 %all-gather.6.cloned.1.call-start = ((), (), s32[]{:S(2)}) async-start(), calls=%async_computation.6 | async-start | bytes 2359296 | tf_op jit(solution)/shard_map/all_gather | solution.py:203
  57.2 30.3 %all-to-all-start = ((bf16[128,32,128]{2,1,0:T(8,128)(2,1)}), bf16[128,32,128]{2,1,0:T(8,128)(2,1)S(1)}, u32[]{:S(2)}, u32[]{:S(2)}) async-start(bf16[128,32,128]{2,1,0:T(8,128)(2,1)} %bitcast.51), calls=%async_computation | async-start | bytes 2097152 | tf_op jit(solution)/shard_map/all_to_all | solution.py:150
  68.4 180.4 %all-gather.8.cloned.1.call-start = ((), (), s32[]{:S(2)}) async-start(), calls=%async_computation.7 | async-start | bytes 2359296 | tf_op jit(solution)/shard_map/all_gather | solution.py:205
  87.5 60.5 %copy-start.7 = (s32[1,8]{1,0:T(1,128)S(1)}, s32[1,8]{1,0:T(1,128)}, u32[]{:S(2)}) copy-start(s32[1,8]{1,0:T(1,128)} %param.22) | copy-start | bytes 100
  87.5 76.8 %copy-start.4 = (bf16[128,2048]{1,0:T(8,128)(2,1)S(1)}, bf16[128,2048]{1,0:T(8,128)(2,1)}, u32[]{:S(2)}) copy-start(bf16[128,2048]{1,0:T(8,128)(2,1)} %param.18) | copy-start | bytes 1572868
  88.9 1.5 copy-start.12
  94.0 1.5 copy-start.12
  99.1 1.5 copy-start.12
  104.3 1.5 copy-start.12
  109.4 1.5 copy-start.12
  114.5 1.5 copy-start.12
  119.7 1.5 copy-start.12
  124.8 1.5 copy-start.12
  129.3 14.0 %all-to-all-start.2 = ((bf16[128,32,1]{1,2,0:T(2,128)(2,1)}), bf16[128,32,1]{1,2,0:T(2,128)(2,1)S(1)}, u32[]{:S(2)}, u32[]{:S(2)}) async-start(bf16[128,32,1]{1,2,0:T(2,128)(2,1)} %reshape.401), calls=%async_computation.2 | async-start | bytes 131072 | tf_op jit(solution)/shard_map/all_to_all | solution.py:162
  143.4 14.0 %all-to-all-start.1 = ((bf16[128,32,1]{1,2,0:T(2,128)(2,1)}), bf16[128,32,1]{1,2,0:T(2,128)(2,1)S(1)}, u32[]{:S(2)}, u32[]{:S(2)}) async-start(bf16[128,32,1]{1,2,0:T(2,128)(2,1)} %reshape.400), calls=%async_computation.1 | async-start | bytes 131072 | tf_op jit(solution)/shard_map/all_to_all | solution.py:161
  157.4 23.7 %all-to-all-start.3 = ((bf16[128,32,128]{2,1,0:T(8,128)(2,1)}), bf16[128,32,128]{2,1,0:T(8,128)(2,1)S(1)}, u32[]{:S(2)}, u32[]{:S(2)}) async-start(bf16[128,32,128]{2,1,0:T(8,128)(2,1)} %bitcast.380), calls=%async_computation.3 | async-start | bytes 2097152 | tf_op jit(solution)/shard_map/all_to_all | solution.py:160
  162.0 138.8 %all-gather.4.cloned.1.call-start = ((), (), s32[]{:S(2)}) async-start(), calls=%async_computation.5 | async-start | bytes 8912896 | tf_op jit(solution)/shard_map/all_gather | solution.py:208
  164.8 1.0 copy-start.5
  228.3 4.4 %copy-start.3 = (bf16[128,2048]{1,0:T(8,128)(2,1)S(1)}, bf16[128,2048]{1,0:T(8,128)(2,1)}, u32[]{:S(2)}) copy-start(bf16[128,2048]{1,0:T(8,128)(2,1)} %param.21) | copy-start | bytes 1572868
  228.3 4.9 %copy-start.8 = (f32[2048]{0:T(1024)S(1)}, f32[2048]{0:T(1024)}, u32[]{:S(2)}) copy-start(f32[2048]{0:T(1024)} %param.31) | copy-start | bytes 24580
  228.3 4.9 %copy-start.9 = (f32[2048]{0:T(1024)S(1)}, f32[2048]{0:T(1024)}, u32[]{:S(2)}) copy-start(f32[2048]{0:T(1024)} %param.30) | copy-start | bytes 24580
  231.1 3.3 copy-start.14
  231.1 4.5 %copy-start.13 = (bf16[64]{0:T(256)(128)(2,1)S(1)}, bf16[64]{0:T(256)(128)(2,1)}, u32[]{:S(2)}) copy-start(bf16[64]{0:T(256)(128)(2,1)} %param.27) | copy-start | bytes 388
  234.3 166.6 %reduce-scatter.2.cloned.1.call-start = ((), (), s32[]{:S(2)}) async-start(), calls=%async_computation.8 | async-start | bytes 8912896 | tf_op jit(solution)/shard_map/reduce_scatter | solution.py:210
  316.0 84.9 %copy-start.2 = (bf16[128,2048]{1,0:T(8,128)(2,1)S(1)}, bf16[128,2048]{1,0:T(8,128)(2,1)}, u32[]{:S(2)}) copy-start(bf16[128,2048]{1,0:T(8,128)(2,1)} %add_convert_fusion.1) | copy-start | bytes 1572868
  316.0 84.9 %copy-start.6 = (f32[2048]{0:T(1024)S(1)}, f32[2048]{0:T(1024)}, u32[]{:S(2)}) copy-start(f32[2048]{0:T(1024)} %param.29) | copy-start | bytes 24580
  316.0 87.6 %copy-start.10 = (f32[2048]{0:T(1024)S(1)}, f32[2048]{0:T(1024)}, u32[]{:S(2)}) copy-start(f32[2048]{0:T(1024)} %param.33) | copy-start | bytes 24580
  316.0 87.6 %copy-start.11 = (f32[2048]{0:T(1024)S(1)}, f32[2048]{0:T(1024)}, u32[]{:S(2)}) copy-start(f32[2048]{0:T(1024)} %param.32) | copy-start | bytes 24580
Sparse Core Ops, SparseCore 0:
  9.1 27.6 all-gather.5
  71.0 26.2 all-gather.7
  234.5 66.3 all-gather.3
  316.2 84.7 reduce-scatter.1
where the time goes:
time: 414 us; the launch traced here: 412 us
  waiting for transfers between devices  186 us (45%)
  local copies, waits for them, and re-layouts  69.7 us (17%)
  matrix products  46.3 us (11%)
  between operations  44.2 us (11%)
  other arithmetic  28.4 us (7%)
  starting transfers between devices  25.1 us (6%)
  blocking collectives  12.8 us (3%)
    reduce_scatter x1, waiting for transfers between devices, on_device(): lax.psum_scatter(jnp.dot(activation, down_slice, preferred_element_type=j...  84.9 us
    all_gather x1, waiting for transfers between devices, on_device(): lax.all_gather(hidden_state, 'dev', axis=0, tiled=True)  52 us
    dynamic_update_slice x8, local copies, waits for them, and re-layouts, on_device(): lax.dynamic_update_slice(placed_answer, own_answer, (starts[request], anc...  40.9 us
    all_to_all x1, waiting for transfers between devices, on_device(): lax.all_to_all(outgoing.reshape(group_count * column_count, capacity, par...  18.3 us
    dot_general x8, matrix products, one_block(): jnp.einsum('hqk,khd->qhd', weights.astype(jnp.bfloat16), value_heads, pre...  17.2 us
    dot_general x1, matrix products, on_device(): jnp.dot(activation, down_slice, preferred_element_type=jnp.float32)  15.2 us
    unnamed x1, blocking collectives  12.8 us
    reduce_sum x8, other arithmetic, one_block(): row_sum = jnp.sum(weights, axis=2)  12 us
  transfers between devices with their start and end apart: 8, of which 6 were waited for; matrix products, arithmetic and copies ran while one was open for 30% of the time, Pallas kernels for 0%

commit v1 on v0

--- a/solution.py
+++ b/solution.py
@@ -6,6 +6,19 @@
 
 HD = 128
 norm_eps = 1e-12
+
+
+def see_the_strings(x_part, mesh_name):
+    r_now = jnp.concatenate(
+        lax.all_to_all(
+            jnp.stack([x_part] * lax.axis_size(mesh_name), 0),
+            split_axis=0,
+            axis_name=mesh_name,
+            concat_axis=0,
+        ),
+        0,
+    )
+    return r_now
 
 
 def layer_norm(summed, norm_gain, norm_shift):
@@ -204,9 +217,7 @@
         lax.all_gather(up_bias, "grp", axis=0, tiled=True),
         lax.all_gather(down_weight, "grp", axis=0, tiled=True),
     )
-    activation = expand_rows(
-        lax.all_gather(hidden_state, "dev", axis=0, tiled=True), up_slice, bias_slice
-    )
+    activation = expand_rows(see_the_strings(hidden_state, "dev"), up_slice, bias_slice)
     mlp_sum = lax.psum_scatter(
         jnp.dot(activation, down_slice, preferred_element_type=jnp.float32).astype(jnp.bfloat16),
         "dev",

time: 414 us -> 504 us (1.22)
  waiting for transfers between devices: 186 us -> 266 us
  starting transfers between devices: 25.1 us -> 30.2 us
    all_to_all x0 -> x1, waiting for transfers between devices: none -> 85.8 us  [see_the_strings(): lax.all_to_all(jnp.stack([x_part] * lax.axis_size(mesh_name), 0), split_a...]
    all_gather x1 -> x0, waiting for transfers between devices: 52 us -> none  [on_device(): lax.all_gather(hidden_state, 'dev', axis=0, tiled=True)]
    all_gather x1, waiting for transfers between devices: 0.02 us -> 27.4 us  [on_device(): lax.all_gather(down_weight, 'grp', axis=0, tiled=True)]
    all_gather x1, waiting for transfers between devices: 0.01 us -> 11 us  [on_device(): lax.all_gather(up_weight, 'grp', axis=1, tiled=True)]
    reduce_scatter x1, waiting for transfers between devices: 84.9 us -> 92.4 us  [on_device(): lax.psum_scatter(jnp.dot(activation, down_slice, preferred_element_type=j...]
  transfers between devices with their start and end apart: 8 -> 8, of which waited for: 6 -> 8; matrix products, arithmetic and copies ran while one was open for 30% -> 2% of each run, Pallas kernels for 0% -> 0%
where the time goes in v1:
time: 504 us; the launch traced here: 502 us
  waiting for transfers between devices  266 us (53%)
  local copies, waits for them, and re-layouts  73.7 us (15%)
  matrix products  46.4 us (9%)
  between operations  44.3 us (9%)
  starting transfers between devices  30.2 us (6%)
  other arithmetic  27.7 us (5%)
  blocking collectives  13.2 us (3%)
    reduce_scatter x1, waiting for transfers between devices, on_device(): lax.psum_scatter(jnp.dot(activation, down_slice, preferred_element_type=j...  92.4 us
    all_to_all x1, waiting for transfers between devices, see_the_strings(): lax.all_to_all(jnp.stack([x_part] * lax.axis_size(mesh_name), 0), split_a...  85.8 us
    dynamic_update_slice x8, local copies, waits for them, and re-layouts, on_device(): lax.dynamic_update_slice(placed_answer, own_answer, (starts[request], anc...  40.9 us
    all_gather x1, waiting for transfers between devices, on_device(): lax.all_gather(down_weight, 'grp', axis=0, tiled=True)  27.4 us
    all_to_all x1, waiting for transfers between devices, on_device(): lax.all_to_all(outgoing.reshape(group_count * column_count, capacity, par...  19 us
    dot_general x8, matrix products, one_block(): jnp.einsum('hqk,khd->qhd', weights.astype(jnp.bfloat16), value_heads, pre...  17.2 us
    dot_general x1, matrix products, on_device(): jnp.dot(activation, down_slice, preferred_element_type=jnp.float32)  15.2 us
    unnamed x1, blocking collectives  13.2 us
  transfers between devices with their start and end apart: 8, of which 8 were waited for; matrix products, arithmetic and copies ran while one was open for 2% of the time, Pallas kernels for 0%

profile of v1, /device:TPU:0, one launch (start us, length us, event | category | flops | bytes accessed | tf_op | source)
XLA Modules:
  0.0 501.9 jit_solution(4496257250069172487)
XLA Ops:
  16.3 1.6 fusion.103
  20.5 1.6 fusion.105
  47.4 1.1 fusion.62
  48.5 1.1 broadcast_in_dim.147
  50.3 1.7 fusion.64
  56.8 11.2 %all-to-all-start = ((bf16[128,32,128]{2,1,0:T(8,128)(2,1)}), bf16[128,32,128]{2,1,0:T(8,128)(2,1)S(1)}, u32[]{:S(2)}, u32[]{:S(2)}) async-start(bf16[128,32,128]{2,1,0:T(8,128)(2,1)} %bitcast.51), calls=%async_computation | async-start | bytes 2097152 | tf_op jit(solution)/shard_map/all_to_all | solution.py:163
  68.0 19.0 %all-to-all-done = bf16[128,32,128]{2,1,0:T(8,128)(2,1)S(1)} async-done(((bf16[128,32,128]{2,1,0:T(8,128)(2,1)}), bf16[128,32,128]{2,1,0:T(8,128)(2,1)S(1)}, u32[]{:S(2)}, u32[]{:S(2)}) %all-to-all-start) | async-done | bytes 1048608 | tf_op jit(solution)/shard_map/all_to_all | solution.py:163
  87.1 41.1 %while.14 = (s32[]{:T(128)}, bf16[8,512,128]{2,1,0:T(8,128)(2,1)}, bf16[8,512,1]{1,0,2:T(8,128)(2,1)S(1)}, bf16[8,512,1]{1,0,2:T(8,128)(2,1)S(1)}, bf16[8,512,1,...) while((s32[]{:T(128)}, bf16[8,512,128]{2,1,0:T(8,128)(2,1)}, ...), condition=%wide.region_4.5_spmd, body=%wide.region_1.4_spmd.sunk | while | flops 1090650112 | bytes 31745668 | solution.py:74
  87.1 1.3 multiply_reduce_fusion.4
  88.4 1.5 fusion.118
  89.9 2.2 fusion.119
  92.2 1.3 multiply_reduce_fusion.4
  93.6 1.5 fusion.118
  95.1 2.1 fusion.119
  97.4 1.3 multiply_reduce_fusion.4
  98.7 1.5 fusion.118
  100.2 2.2 fusion.119
  102.5 1.3 multiply_reduce_fusion.4
  103.9 1.5 fusion.118
  105.4 2.1 fusion.119
  107.6 1.3 multiply_reduce_fusion.4
  109.0 1.5 fusion.118
  110.5 2.1 fusion.119
  112.8 1.3 multiply_reduce_fusion.4
  114.2 1.5 fusion.118
  115.7 2.1 fusion.119
  117.9 1.3 multiply_reduce_fusion.4
  119.3 1.5 fusion.118
  120.8 2.1 fusion.119
  123.1 1.3 multiply_reduce_fusion.4
  124.4 1.5 fusion.118
  125.9 2.2 fusion.119
  128.9 4.6 all-to-all-start.1
  134.3 8.7 %all-to-all-done.1 = bf16[128,32,1]{1,2,0:T(2,128)(2,1)S(1)} async-done(((bf16[128,32,1]{1,2,0:T(2,128)(2,1)}), bf16[128,32,1]{1,2,0:T(2,128)(2,1)S(1)}, u32[]{:S(2)}, u32[]{:S(2)}) %all-to-all-start.1) | async-done | bytes 8224 | tf_op jit(solution)/shard_map/all_to_all | solution.py:174
  142.9 4.6 all-to-all-start.2
  147.6 9.4 %all-to-all-done.2 = bf16[128,32,1]{1,2,0:T(2,128)(2,1)S(1)} async-done(((bf16[128,32,1]{1,2,0:T(2,128)(2,1)}), bf16[128,32,1]{1,2,0:T(2,128)(2,1)S(1)}, u32[]{:S(2)}, u32[]{:S(2)}) %all-to-all-start.2) | async-done | bytes 8224 | tf_op jit(solution)/shard_map/all_to_all | solution.py:175
  157.0 4.8 all-to-all-start.3
  161.9 2.0 copy.149
  169.9 10.8 %all-to-all-done.3 = bf16[128,32,128]{2,1,0:T(8,128)(2,1)S(1)} async-done(((bf16[128,32,128]{2,1,0:T(8,128)(2,1)}), bf16[128,32,128]{2,1,0:T(8,128)(2,1)S(1)}, u32[]{:S(2)}, u32[]{:S(2)}) %all-to-all-start.3) | async-done | bytes 1048608 | tf_op jit(solution)/shard_map/all_to_all | solution.py:173
  180.8 1.0 copy.137
  182.8 1.0 copy.139
  183.9 1.0 copy.140
  184.9 1.0 copy.141
  186.9 4.9 dynamic_update_slice.131
  191.8 5.9 %dynamic_update_slice.132 = bf16[160,2048]{0,1:T(8,128)(2,1)S(1)} dynamic-update-slice(bf16[160,2048]{0,1:T(8,128)(2,1)S(1)} %dynamic_update_slice.131, bf16[32,2048]{0,1:T(8,128)(2,1)} %bitcast.379, s32[]{:T(128)S(6)} %select_n.137, s32[]{:T(128)} %constant.96.clone.1) | dynamic-update-slice | bytes 262148 | tf_op jit(solution)/shard_map/dynamic_update_slice | solution.py:198
  197.7 5.9 %dynamic_update_slice.133 = bf16[160,2048]{0,1:T(8,128)(2,1)S(1)} dynamic-update-slice(bf16[160,2048]{0,1:T(8,128)(2,1)S(1)} %dynamic_update_slice.132, bf16[32,2048]{0,1:T(8,128)(2,1)} %bitcast.378, s32[]{:T(128)S(6)} %select_n.140, s32[]{:T(128)} %constant.96.clone.1) | dynamic-update-slice | bytes 262148 | tf_op jit(solution)/shard_map/dynamic_update_slice | solution.py:198
  203.7 5.9 %dynamic_update_slice.134 = bf16[160,2048]{0,1:T(8,128)(2,1)S(1)} dynamic-update-slice(bf16[160,2048]{0,1:T(8,128)(2,1)S(1)} %dynamic_update_slice.133, bf16[32,2048]{0,1:T(8,128)(2,1)} %bitcast.377, s32[]{:T(128)S(6)} %select_n.143, s32[]{:T(128)} %constant.96.clone.1) | dynamic-update-slice | bytes 262148 | tf_op jit(solution)/shard_map/dynamic_update_slice | solution.py:198
  209.6 5.9 %dynamic_update_slice.135 = bf16[160,2048]{0,1:T(8,128)(2,1)S(1)} dynamic-update-slice(bf16[160,2048]{0,1:T(8,128)(2,1)S(1)} %dynamic_update_slice.134, bf16[32,2048]{0,1:T(8,128)(2,1)} %bitcast.376, s32[]{:T(128)S(6)} %select_n.146, s32[]{:T(128)} %constant.96.clone.1) | dynamic-update-slice | bytes 262148 | tf_op jit(solution)/shard_map/dynamic_update_slice | solution.py:198
  215.6 4.0 dynamic_update_slice.136
  219.6 4.0 dynamic_update_slice.137
  223.6 4.2 dynamic_update_slice.138
  227.9 2.8 fusion.36
  230.7 1.6 copy.147
  233.1 4.3 stack.2
  237.5 4.9 all-to-all-start.4
  245.4 13.2 %all-reduce.1 = bf16[512]{0:T(512)(128)(2,1)S(1)} all-reduce(bf16[512]{0:T(512)(128)(2,1)S(1)} %dynamic-update-slice), channel_id=1, replica_groups=mesh['grp'=8,'dev'=16] {'grp'}, use_global_device_ids=true, to_apply=%add.1 | all-reduce | flops 512 | bytes 2048
  258.6 11.0 %all-gather.3.cloned.1.call-done = bf16[2048,512]{0,1:T(8,128)(2,1)} async-done(((bf16[2048,64]{0,1:T(8,128)(2,1)}), bf16[2048,512]{0,1:T(8,128)(2,1)}) %all-gather.3.cloned.1.call-update) | async-done | bytes 2097168 | tf_op jit(solution)/shard_map/all_gather | solution.py:216
  269.7 27.4 %all-gather.5.cloned.1.call-done = bf16[512,2048]{1,0:T(8,128)(2,1)} async-done(((bf16[64,2048]{1,0:T(8,128)(2,1)}), bf16[512,2048]{1,0:T(8,128)(2,1)}) %all-gather.5.cloned.1.call-update) | async-done | bytes 2097168 | tf_op jit(solution)/shard_map/all_gather | solution.py:218
  297.1 85.8 %all-to-all-done.4 = bf16[16,128,2048]{2,1,0:T(8,128)(2,1)} async-done(((bf16[16,128,2048]{2,1,0:T(8,128)(2,1)}), bf16[16,128,2048]{2,1,0:T(8,128)(2,1)}, u32[]{:S(2)}, u32[]{:S(2)}) %all-to-all-start.4) | async-done | bytes 8388640 | tf_op jit(solution)/shard_map/all_to_all | solution.py:13
  382.8 15.2 %convolution_convert_fusion = bf16[2048,2048]{1,0:T(8,128)(2,1)} fusion(bf16[512,2048]{1,0:T(8,128)(2,1)} %all-gather.5.cloned.1.call-done, bf16[2048,2048]{1,0:T(8,128)(2,1)} %bitcast.138, bf16[2048,512]{0,1:T(8,128)(2,1)} %all-gather.3.cloned.1.call-done, f32[512]{0:T(512)S(1)} %convert_element_type.97), kind=kOutput, calls=%fused_computation.17 | convolution fusion | flops 8604614656 | bytes 20973568 | tf_op jit(solution)/shard_map/dot_general | solution.py:222
  398.1 92.4 %reduce-scatter.2.cloned.1.call-done = bf16[128,2048]{1,0:T(8,128)(2,1)} async-done(((bf16[2048,2048]{1,0:T(8,128)(2,1)}), bf16[128,2048]{1,0:T(8,128)(2,1)}) %reduce-scatter.2.cloned.1.call-update) | async-done | bytes 524304 | tf_op jit(solution)/shard_map/reduce_scatter | solution.py:221
  490.5 1.3 fusion.39
  491.8 1.4 multiply_reduce_fusion.1
  493.2 2.2 add_convert_fusion
  (173 shorter events, 26.4 us)
Async XLA Ops:
  6.5 157.5 %copy-start = (bf16[128,2048]{1,0:T(8,128)(2,1)S(1)}, bf16[128,2048]{1,0:T(8,128)(2,1)}, u32[]{:S(2)}) copy-start(bf16[128,2048]{1,0:T(8,128)(2,1)} %param.19) | copy-start | bytes 1572868
  6.5 80.5 %copy-start.1 = (bf16[1,4096,128]{2,1,0:T(8,128)(2,1)S(1)}, bf16[1,4096,128]{2,1,0:T(8,128)(2,1)}, u32[]{:S(2)}) copy-start(bf16[1,4096,128]{2,1,0:T(8,128)(2,1)} %param.24) | copy-start | bytes 3145732
  56.8 30.3 %all-to-all-start = ((bf16[128,32,128]{2,1,0:T(8,128)(2,1)}), bf16[128,32,128]{2,1,0:T(8,128)(2,1)S(1)}, u32[]{:S(2)}, u32[]{:S(2)}) async-start(bf16[128,32,128]{2,1,0:T(8,128)(2,1)} %bitcast.51), calls=%async_computation | async-start | bytes 2097152 | tf_op jit(solution)/shard_map/all_to_all | solution.py:163
  87.1 60.5 %copy-start.6 = (s32[1,8]{1,0:T(1,128)S(1)}, s32[1,8]{1,0:T(1,128)}, u32[]{:S(2)}) copy-start(s32[1,8]{1,0:T(1,128)} %param.22) | copy-start | bytes 100
  87.1 77.0 %copy-start.3 = (bf16[128,2048]{1,0:T(8,128)(2,1)S(1)}, bf16[128,2048]{1,0:T(8,128)(2,1)}, u32[]{:S(2)}) copy-start(bf16[128,2048]{1,0:T(8,128)(2,1)} %param.18) | copy-start | bytes 1572868
  88.4 1.5 copy-start.11
  93.6 1.5 copy-start.11
  98.7 1.5 copy-start.11
  103.9 1.5 copy-start.11
  109.0 1.5 copy-start.11
  114.1 1.5 copy-start.11
  119.3 1.5 copy-start.11
  124.4 1.5 copy-start.11
  128.9 14.0 %all-to-all-start.1 = ((bf16[128,32,1]{1,2,0:T(2,128)(2,1)}), bf16[128,32,1]{1,2,0:T(2,128)(2,1)S(1)}, u32[]{:S(2)}, u32[]{:S(2)}) async-start(bf16[128,32,1]{1,2,0:T(2,128)(2,1)} %reshape.406), calls=%async_computation.1 | async-start | bytes 131072 | tf_op jit(solution)/shard_map/all_to_all | solution.py:174
  142.9 14.1 %all-to-all-start.2 = ((bf16[128,32,1]{1,2,0:T(2,128)(2,1)}), bf16[128,32,1]{1,2,0:T(2,128)(2,1)S(1)}, u32[]{:S(2)}, u32[]{:S(2)}) async-start(bf16[128,32,1]{1,2,0:T(2,128)(2,1)} %reshape.407), calls=%async_computation.2 | async-start | bytes 131072 | tf_op jit(solution)/shard_map/all_to_all | solution.py:175
  157.0 23.7 %all-to-all-start.3 = ((bf16[128,32,128]{2,1,0:T(8,128)(2,1)}), bf16[128,32,128]{2,1,0:T(8,128)(2,1)S(1)}, u32[]{:S(2)}, u32[]{:S(2)}) async-start(bf16[128,32,128]{2,1,0:T(8,128)(2,1)} %bitcast.381), calls=%async_computation.3 | async-start | bytes 2097152 | tf_op jit(solution)/shard_map/all_to_all | solution.py:173
  164.6 1.0 copy-start.4
  227.9 4.4 copy-start.2
  227.9 4.9 copy-start.7
  227.9 4.9 copy-start.8
  237.4 6.4 %copy-start.13 = (u32[128]{0:T(128)S(1)}, u32[128]{0:T(128)}, u32[]{:S(2)}) copy-start(u32[128]{0:T(128)} %constant.119) | copy-start | bytes 1540
  237.4 7.7 %copy-start.12 = (bf16[64]{0:T(256)(128)(2,1)S(1)}, bf16[64]{0:T(256)(128)(2,1)}, u32[]{:S(2)}) copy-start(bf16[64]{0:T(256)(128)(2,1)} %param.27) | copy-start | bytes 388
  237.5 145.4 %all-to-all-start.4 = ((bf16[16,128,2048]{2,1,0:T(8,128)(2,1)}), bf16[16,128,2048]{2,1,0:T(8,128)(2,1)}, u32[]{:S(2)}, u32[]{:S(2)}) async-start(bf16[16,128,2048]{2,1,0:T(8,128)(2,1)} %stack.2), calls=%async_computation.4 | async-start | bytes 16777216 | tf_op jit(solution)/shard_map/all_to_all | solution.py:13
  242.3 27.3 %all-gather.3.cloned.1.call-start = ((), (), s32[]{:S(2)}) async-start(), calls=%async_computation.6 | async-start | bytes 2359296 | tf_op jit(solution)/shard_map/all_gather | solution.py:216
  243.1 54.0 %all-gather.5.cloned.1.call-start = ((), (), s32[]{:S(2)}) async-start(), calls=%async_computation.7 | async-start | bytes 2359296 | tf_op jit(solution)/shard_map/all_gather | solution.py:218
  243.8 246.6 %reduce-scatter.2.cloned.1.call-start = ((), (), s32[]{:S(2)}) async-start(), calls=%async_computation.8 | async-start | bytes 8912896 | tf_op jit(solution)/shard_map/reduce_scatter | solution.py:221
  398.0 92.4 %copy-start.5 = (f32[2048]{0:T(1024)S(1)}, f32[2048]{0:T(1024)}, u32[]{:S(2)}) copy-start(f32[2048]{0:T(1024)} %param.29) | copy-start | bytes 24580
  398.0 95.1 %copy-start.9 = (f32[2048]{0:T(1024)S(1)}, f32[2048]{0:T(1024)}, u32[]{:S(2)}) copy-start(f32[2048]{0:T(1024)} %param.33) | copy-start | bytes 24580
  398.0 95.1 %copy-start.10 = (f32[2048]{0:T(1024)S(1)}, f32[2048]{0:T(1024)}, u32[]{:S(2)}) copy-start(f32[2048]{0:T(1024)} %param.32) | copy-start | bytes 24580
Sparse Core Ops, SparseCore 0:
  244.9 24.7 all-gather.2
  271.4 25.6 all-gather.4
  398.2 92.2 reduce-scatter.1
